TPU v7x, 32 devices: a whole 2x2x4 slice. The times are simulated.
32 devices in a mesh: tm: 2 (over x), grid: 16 (over z, y, core).
Axes of the slice: x: 2, y: 2, z: 4, core: 2. Of those that a mesh axis runs over, the one named last changes fastest.
Arguments:
- occupied_green: bfloat16 [2, 1024, 1024], P('tm', 'grid'), may hold values from -0.005859375 to 0.005859375
- empty_green: bfloat16 [2, 1024, 1024], P('tm', 'grid'), may hold values from -0.005859375 to 0.005859375
- basis: bfloat16 [12288, 1024], P('grid'), may hold values from -8 to 8
- time_weights: float32 [2, 2], replicated, may hold values from 0.25 to 1
Outputs:
- polarizability: float32 [2, 1024, 1024], P('tm', 'grid')
All inputs are finite; a program needn't handle non-finite values.
Results may differ from a plain program's by a relative error of at most 0.0012.
Values may be sent and summed in bfloat16 or wider, within the bound.
A program may use at most 128 MiB of HBM per device.

v0:
```python
import jax
import jax.numpy as jnp
from jax import lax
from jax.sharding import PartitionSpec as P

NR = 12288
NB = 1024


def weigh_times(time_weights, block_list, scale_factor):
    time_count = len(block_list)
    group_index = lax.axis_index("tm")
    weights_local = lax.dynamic_slice_in_dim(time_weights, group_index * time_count, time_count, 1)
    accum = weights_local[:, 0, None, None] * block_list[0][None]
    return scale_factor * accum


def step_size(piece_rows):
    return max((divisor for divisor in range(1, 2049) if piece_rows % divisor == 0))


def shards(occupied_green, empty_green, basis, time_weights):
    stacked = jnp.stack([occupied_green, empty_green])
    time_count = occupied_green.shape[0]
    coef_block = occupied_green.shape[1]
    row_total = basis.shape[0]
    scale_factor = 1.0 / NR

    def make_accumulate(combined_rows):

        def accumulate(running, basis_piece, first_row):
            piece_rows = basis_piece.shape[0]
            step_rows = step_size(piece_rows)

            def one_step(step_index, inner):
                basis_subpart = lax.dynamic_slice_in_dim(
                    basis_piece, step_index * step_rows, step_rows, 0
                )
                real_pair = jnp.einsum(
                    "qoa,ba->qob", combined_rows, basis_subpart, preferred_element_type=jnp.float32
                )
                product = (real_pair[0] * real_pair[1]).astype(jnp.bfloat16)
                return inner + jnp.dot(product, basis_subpart, preferred_element_type=jnp.float32)

            return lax.fori_loop(0, piece_rows // step_rows, one_step, running)

        return accumulate

    initial = jnp.zeros((time_count * row_total, NB), jnp.float32)
    projected = jnp.einsum(
        "sl,ftkl->ftsk",
        basis,
        lax.all_gather(stacked, "grid", axis=2, tiled=True),
        preferred_element_type=jnp.float32,
    ).astype(jnp.bfloat16)
    combined_rows = projected.reshape(2, time_count * row_total, NB)
    accumulate = make_accumulate(combined_rows)
    summed = accumulate(initial, lax.all_gather(basis, "grid", axis=0, tiled=True), jnp.int32(0))
    back_half = summed.astype(jnp.bfloat16).reshape(time_count, row_total, NB)
    coef_rows = lax.psum_scatter(
        jnp.einsum("tsk,sl->ktl", back_half, basis, preferred_element_type=jnp.float32).reshape(
            lax.axis_size("grid") * coef_block, time_count * NB
        ),
        "grid",
        scatter_dimension=0,
        tiled=True,
    ).reshape(coef_block, time_count, NB)
    block_list = [coef_rows[:, 0]]
    result = lax.psum_scatter(
        weigh_times(time_weights, block_list, scale_factor), "tm", scatter_dimension=0, tiled=True
    )
    return result


def solution(mesh):
    in_specs = (P("tm", "grid", None), P("tm", "grid", None), P("grid", None), P())
    out_specs = P("tm", "grid", None)
    return jax.shard_map(shards, mesh=mesh, in_specs=in_specs, out_specs=out_specs, check_vma=False)
```

profile of v0, /device:TPU:0, one launch (start us, length us, event | category | flops | bytes accessed | tf_op | source)
XLA Modules:
  0.0 431.6 jit_solution(16188916720244867342)
XLA Ops:
  6.5 1.7 pad_maximum_fusion
  8.3 0.7 all-gather.3.cloned.1.call-update
  9.1 53.6 %all-gather.5.cloned.1.call-done = bf16[2,1,1024,1024]{3,2,0,1:T(8,128)(2,1)} async-done(((bf16[2,1,64,1024]{3,2,0,1:T(8,128)(2,1)}), bf16[2,1,1024,1024]{3,2,0,1:T(8,128)(2,1)}) %all-gather.5.cloned.1.call-update) | async-done | bytes 4194320 | tf_op jit(solution)/shard_map/all_gather | solution.py:53
  62.7 7.9 %convert_bitcast_fusion = bf16[2,768,1024]{1,2,0:T(8,128)(2,1)} fusion(bf16[2,1,1024,1024]{3,2,0,1:T(8,128)(2,1)} %all-gather.5.cloned.1.call-done, bf16[768,1024]{1,0:T(8,128)(2,1)} %param.8), kind=kOutput, calls=%fused_computation.13 | convolution fusion | flops 3222798336 | bytes 8912896 | tf_op jit(solution)/shard_map/sl,ftkl->ftsk/dot_general | solution.py:50
  70.5 3.2 copy.5
  73.8 117.6 %all-gather.3.cloned.1.call-done = bf16[12288,1024]{1,0:T(8,128)(2,1)} async-done(((bf16[768,1024]{1,0:T(8,128)(2,1)}), bf16[12288,1024]{1,0:T(8,128)(2,1)}) %all-gather.3.cloned.1.call-update) | async-done | bytes 25165840 | tf_op jit(solution)/shard_map/all_gather | solution.py:58
  191.3 138.8 %while.14 = (s32[]{:T(128)}, f32[768,1024]{1,0:T(8,128)}, bf16[12288,1024]{1,0:T(8,128)(2,1)}, bf16[2,768,1024]{2,1,0:T(8,128)(2,1)S(1)}, s32[]{:T(128)}, /*index=5*/s32[]{:T(128)}, s32[]{:T(128)}, s32[]{:T(128)}) while((s32[]{:T(128)}, f32[768,1024]{1,0:T(8,128)}, bf16[12288,1024]{1,0:T(8,128)(2,1)}, ...), condition=%wide.region_1.0_spmd.clone, body=%wide.region_0.0_spmd.clone.sunk | while | flops 9668395008 | bytes 42991772 | solution.py:45
  191.4 11.5 %convolution_bitcast_fusion.2 = f32[2,768,2048]{1,2,0:T(8,128)} fusion(bf16[2,768,1024]{2,1,0:T(8,128)(2,1)S(1)} %get-tuple-element.156, bf16[12288,1024]{1,0:T(8,128)(2,1)} %get-tuple-element.155, s32[]{:T(128)S(6)} %select_n.13), kind=kOutput, calls=%fused_computation.2.clone.1 | convolution fusion | flops 6442450944 | bytes 19922948 | tf_op jit(solution)/shard_map/while/body/eval_jaxpr/qoa,ba->qob/dot_general | solution.py:39
  202.9 10.9 %select_add_fusion.2 = f32[768,1024]{1,0:T(8,128)} fusion(f32[768,1024]{1,0:T(8,128)} %get-tuple-element.146, bf16[12288,1024]{1,0:T(8,128)(2,1)} %get-tuple-element.155, s32[]{:T(128)S(6)} %select_n.13, f32[2,768,2048]{1,2,0:T(8,128)} %convolution_bitcast_fusion.2, pred[]{:T(512)S(6)} %compare.3), kind=kOutput, calls=%fused_computation.8.clone.1 | convolution fusion | flops 3225944064 | bytes 23068676 | tf_op jit(solution)/shard_map/while/body/eval_jaxpr/dot_general | solution.py:43
  213.7 11.5 %convolution_bitcast_fusion.2 = f32[2,768,2048]{1,2,0:T(8,128)} fusion(bf16[2,768,1024]{2,1,0:T(8,128)(2,1)S(1)} %get-tuple-element.156, bf16[12288,1024]{1,0:T(8,128)(2,1)} %get-tuple-element.155, s32[]{:T(128)S(6)} %select_n.13), kind=kOutput, calls=%fused_computation.2.clone.1 | convolution fusion | flops 6442450944 | bytes 19922948 | tf_op jit(solution)/shard_map/while/body/eval_jaxpr/qoa,ba->qob/dot_general | solution.py:39
  225.2 11.8 %select_add_fusion.2 = f32[768,1024]{1,0:T(8,128)} fusion(f32[768,1024]{1,0:T(8,128)} %get-tuple-element.146, bf16[12288,1024]{1,0:T(8,128)(2,1)} %get-tuple-element.155, s32[]{:T(128)S(6)} %select_n.13, f32[2,768,2048]{1,2,0:T(8,128)} %convolution_bitcast_fusion.2, pred[]{:T(512)S(6)} %compare.3), kind=kOutput, calls=%fused_computation.8.clone.1 | convolution fusion | flops 3225944064 | bytes 23068676 | tf_op jit(solution)/shard_map/while/body/eval_jaxpr/dot_general | solution.py:43
  237.0 11.5 %convolution_bitcast_fusion.2 = f32[2,768,2048]{1,2,0:T(8,128)} fusion(bf16[2,768,1024]{2,1,0:T(8,128)(2,1)S(1)} %get-tuple-element.156, bf16[12288,1024]{1,0:T(8,128)(2,1)} %get-tuple-element.155, s32[]{:T(128)S(6)} %select_n.13), kind=kOutput, calls=%fused_computation.2.clone.1 | convolution fusion | flops 6442450944 | bytes 19922948 | tf_op jit(solution)/shard_map/while/body/eval_jaxpr/qoa,ba->qob/dot_general | solution.py:39
  248.5 11.8 %select_add_fusion.2 = f32[768,1024]{1,0:T(8,128)} fusion(f32[768,1024]{1,0:T(8,128)} %get-tuple-element.146, bf16[12288,1024]{1,0:T(8,128)(2,1)} %get-tuple-element.155, s32[]{:T(128)S(6)} %select_n.13, f32[2,768,2048]{1,2,0:T(8,128)} %convolution_bitcast_fusion.2, pred[]{:T(512)S(6)} %compare.3), kind=kOutput, calls=%fused_computation.8.clone.1 | convolution fusion | flops 3225944064 | bytes 23068676 | tf_op jit(solution)/shard_map/while/body/eval_jaxpr/dot_general | solution.py:43
  260.3 11.5 %convolution_bitcast_fusion.2 = f32[2,768,2048]{1,2,0:T(8,128)} fusion(bf16[2,768,1024]{2,1,0:T(8,128)(2,1)S(1)} %get-tuple-element.156, bf16[12288,1024]{1,0:T(8,128)(2,1)} %get-tuple-element.155, s32[]{:T(128)S(6)} %select_n.13), kind=kOutput, calls=%fused_computation.2.clone.1 | convolution fusion | flops 6442450944 | bytes 19922948 | tf_op jit(solution)/shard_map/while/body/eval_jaxpr/qoa,ba->qob/dot_general | solution.py:39
  271.8 11.8 %select_add_fusion.2 = f32[768,1024]{1,0:T(8,128)} fusion(f32[768,1024]{1,0:T(8,128)} %get-tuple-element.146, bf16[12288,1024]{1,0:T(8,128)(2,1)} %get-tuple-element.155, s32[]{:T(128)S(6)} %select_n.13, f32[2,768,2048]{1,2,0:T(8,128)} %convolution_bitcast_fusion.2, pred[]{:T(512)S(6)} %compare.3), kind=kOutput, calls=%fused_computation.8.clone.1 | convolution fusion | flops 3225944064 | bytes 23068676 | tf_op jit(solution)/shard_map/while/body/eval_jaxpr/dot_general | solution.py:43
  283.6 11.5 %convolution_bitcast_fusion.2 = f32[2,768,2048]{1,2,0:T(8,128)} fusion(bf16[2,768,1024]{2,1,0:T(8,128)(2,1)S(1)} %get-tuple-element.156, bf16[12288,1024]{1,0:T(8,128)(2,1)} %get-tuple-element.155, s32[]{:T(128)S(6)} %select_n.13), kind=kOutput, calls=%fused_computation.2.clone.1 | convolution fusion | flops 6442450944 | bytes 19922948 | tf_op jit(solution)/shard_map/while/body/eval_jaxpr/qoa,ba->qob/dot_general | solution.py:39
  295.1 11.8 %select_add_fusion.2 = f32[768,1024]{1,0:T(8,128)} fusion(f32[768,1024]{1,0:T(8,128)} %get-tuple-element.146, bf16[12288,1024]{1,0:T(8,128)(2,1)} %get-tuple-element.155, s32[]{:T(128)S(6)} %select_n.13, f32[2,768,2048]{1,2,0:T(8,128)} %convolution_bitcast_fusion.2, pred[]{:T(512)S(6)} %compare.3), kind=kOutput, calls=%fused_computation.8.clone.1 | convolution fusion | flops 3225944064 | bytes 23068676 | tf_op jit(solution)/shard_map/while/body/eval_jaxpr/dot_general | solution.py:43
  306.9 11.5 %convolution_bitcast_fusion.2 = f32[2,768,2048]{1,2,0:T(8,128)} fusion(bf16[2,768,1024]{2,1,0:T(8,128)(2,1)S(1)} %get-tuple-element.156, bf16[12288,1024]{1,0:T(8,128)(2,1)} %get-tuple-element.155, s32[]{:T(128)S(6)} %select_n.13), kind=kOutput, calls=%fused_computation.2.clone.1 | convolution fusion | flops 6442450944 | bytes 19922948 | tf_op jit(solution)/shard_map/while/body/eval_jaxpr/qoa,ba->qob/dot_general | solution.py:39
  318.4 11.8 %select_add_fusion.2 = f32[768,1024]{1,0:T(8,128)} fusion(f32[768,1024]{1,0:T(8,128)} %get-tuple-element.146, bf16[12288,1024]{1,0:T(8,128)(2,1)} %get-tuple-element.155, s32[]{:T(128)S(6)} %select_n.13, f32[2,768,2048]{1,2,0:T(8,128)} %convolution_bitcast_fusion.2, pred[]{:T(512)S(6)} %compare.3), kind=kOutput, calls=%fused_computation.8.clone.1 | convolution fusion | flops 3225944064 | bytes 23068676 | tf_op jit(solution)/shard_map/while/body/eval_jaxpr/dot_general | solution.py:43
  330.2 6.1 %fusion.18 = f32[1024,1024]{1,0:T(8,128)} fusion(bf16[768,1024]{1,0:T(8,128)(2,1)} %param.8, f32[768,1024]{1,0:T(8,128)} %get-tuple-element.84), kind=kOutput, calls=%fused_computation.15 | convolution fusion | flops 1611399168 | bytes 8912896 | tf_op jit(solution)/shard_map/tsk,sl->ktl/dot_general | solution.py:61
  336.4 0.2 dynamic-slice_reduce_fusion
  336.6 72.7 %reduce-scatter.3.cloned.1.call-done = f32[64,1024]{1,0:T(8,128)} async-done(((f32[1024,1024]{1,0:T(8,128)}), f32[64,1024]{1,0:T(8,128)}) %reduce-scatter.3.cloned.1.call-update) | async-done | bytes 262160 | tf_op jit(solution)/shard_map/reduce_scatter | solution.py:60
  409.2 1.9 multiply_multiply_fusion
  411.1 13.9 %reduce-scatter.5.cloned.1.call-done = f32[1,64,1024]{2,1,0:T(8,128)} async-done(((f32[2,64,1024]{2,1,0:T(8,128)}), f32[1,64,1024]{2,1,0:T(8,128)}) %reduce-scatter.5.cloned.1.call-update) | async-done | bytes 262160 | tf_op jit(solution)/shard_map/reduce_scatter | solution.py:69
  (10 shorter events, 0.2 us)
Async XLA Ops:
  6.5 329.8 %copy-start = (f32[2,2]{1,0:T(2,128)S(1)}, f32[2,2]{1,0:T(2,128)}, u32[]{:S(2)}) copy-start(f32[2,2]{1,0:T(2,128)} %param.9) | copy-start | bytes 52
  6.5 56.1 %all-gather.5.cloned.1.call-start = ((), (), s32[]{:S(2)}) async-start(), calls=%async_computation.3 | async-start | bytes 4456448 | tf_op jit(solution)/shard_map/all_gather | solution.py:53
  8.3 183.1 %all-gather.3.cloned.1.call-start = ((), (), s32[]{:S(2)}) async-start(), calls=%async_computation.2 | async-start | bytes 26738688 | tf_op jit(solution)/shard_map/all_gather | solution.py:58
  9.0 400.2 %reduce-scatter.3.cloned.1.call-start = ((), (), s32[]{:S(2)}) async-start(), calls=%async_computation.4 | async-start | bytes 4456448 | tf_op jit(solution)/shard_map/reduce_scatter | solution.py:60
  336.3 88.8 %reduce-scatter.5.cloned.1.call-start = ((), (), s32[]{:S(2)}) async-start(), calls=%async_computation.5 | async-start | bytes 786432 | tf_op jit(solution)/shard_map/reduce_scatter | solution.py:69
Sparse Core Ops, SparseCore 0:
  9.5 53.1 all-gather.4
  64.3 127.0 all-gather.2
  336.4 72.7 reduce-scatter.2
  411.3 13.6 reduce-scatter.4
where the time goes:
time: 432 us
  waiting for transfers between devices  259 us (60%)
  matrix products  153 us (35%)
  between operations  13.2 us (3%)
    all_gather x1, waiting for transfers between devices, shards(): lax.all_gather(basis, 'grid', axis=0, tiled=True)  118 us
    reduce_scatter x1, waiting for transfers between devices, shards(): lax.psum_scatter(jnp.einsum('tsk,sl->ktl', back_half, basis, preferred_el...  72.7 us
    dot_general x6, matrix products, one_step(): jnp.dot(product, basis_subpart, preferred_element_type=jnp.float32)  69.8 us
    dot_general x6, matrix products, one_step(): jnp.einsum('qoa,ba->qob', combined_rows, basis_subpart, preferred_element...  69 us
    all_gather x1, waiting for transfers between devices, shards(): lax.all_gather(stacked, 'grid', axis=2, tiled=True)  53.6 us
    reduce_scatter x1, waiting for transfers between devices, shards(): lax.psum_scatter(weigh_times(time_weights, block_list, scale_factor), 'tm...  13.9 us
  transfers between devices with their start and end apart: 4, of which 4 were waited for; matrix products, arithmetic and copies ran while one was open for 3% of the time, Pallas kernels for 0%

commit v1 on v0

v1 whole, which is shorter than its diff:
```python
import functools

import jax
import jax.numpy as jnp
from jax import lax
from jax.experimental import pallas as pl
from jax.experimental.pallas import tpu as pltpu
from jax.sharding import PartitionSpec as P

MESH = pl.DeviceIdType.MESH
NT = (((1,), (1,)), ((), ()))
TN = (((0,), (0,)), ((), ()))


def tile_of(total, most):
    return max(d for d in range(1, most + 1) if total % d == 0)


def kernel(
    nc, nr, occ_ref, emp_ref, basis_ref, w_ref, out_ref,
    full, green, proj, acc, part, half, sums, twin,
    load_sem, gs_ring, gr_ring, gs_loc, gr_loc,
    s_ring, r_ring, s_x, r_x, s_loc, r_loc,
    cs_sem, cr_sem, ss_sem, sr_sem, ts_sem, tr_sem,
):
    tm = lax.axis_index("tm")
    me = lax.axis_index("grid")
    rows, nb = basis_ref.shape
    kb = occ_ref.shape[1]
    core = lax.rem(me, 2)
    chip = me // 2
    side = lax.rem(chip, 2)
    lane = chip // 2
    pos = (1 - side) * lane + side * (nc - 1 - lane)
    step_dir = 1 - 2 * core

    def chip_at(position):
        q = lax.rem(position + 2 * nc, nc)
        far = q // (nc // 2)
        return (1 - far) * 2 * q + far * (2 * (nc - 1 - q) + 1)

    def block_at(hops, which_core):
        direction = 1 - 2 * which_core
        return 2 * chip_at(pos - direction * hops) + which_core

    nxt = (tm, 2 * chip_at(pos + step_dir) + core)
    prv = (tm, 2 * chip_at(pos - step_dir) + core)
    mate = (tm, me + step_dir)
    other = (1 - tm, me)
    mate_core = 1 - core

    def remote(src, dst, send, recv, dev):
        return pltpu.make_async_remote_copy(
            src_ref=src, dst_ref=dst, send_sem=send, recv_sem=recv, device_id=dev, device_id_type=MESH
        )

    loads = [
        pltpu.make_async_copy(occ_ref.at[0], green.at[me, 0], load_sem.at[0]),
        pltpu.make_async_copy(emp_ref.at[0], green.at[me, 1], load_sem.at[1]),
        pltpu.make_async_copy(basis_ref, full.at[me], load_sem.at[2]),
    ]
    for load in loads:
        load.start()

    barrier = pltpu.get_barrier_semaphore()
    for peer in (nxt, prv, mate, other):
        pl.semaphore_signal(barrier, inc=1, device_id=peer, device_id_type=MESH)
    pl.semaphore_wait(barrier, 4)

    def g_ring(hops, u):
        b = block_at(hops, core)
        return remote(green.at[b, u], green.at[b, u], gs_ring.at[2 * hops + u], gr_ring.at[2 * hops + u], nxt)

    def g_loc(hops, u, which_core):
        b = block_at(hops, which_core)
        return remote(green.at[b, u], green.at[b, u], gs_loc.at[2 * hops + u], gr_loc.at[2 * hops + u], mate)

    def g_arrived(hops, u):
        b = block_at(hops, core)
        return remote(
            green.at[b, u], green.at[b, u], gs_ring.at[2 * (hops - 1) + u], gr_ring.at[2 * (hops - 1) + u], nxt
        )

    third = rows // 3

    def piece(b, t):
        return full.at[b, pl.ds(pl.multiple_of(t * third, 16), third)]

    def third_of(u):
        return (2 * tm, 1, 2 - 2 * tm)[u]

    def b_ring(hops, u, src_hops):
        ref = piece(block_at(src_hops, core), third_of(u))
        return remote(ref, ref, s_ring.at[2 * hops + u], r_ring.at[2 * hops + u], nxt)

    def b_x(hops, u):
        ref = piece(block_at(hops, core), third_of(u))
        return remote(ref, ref, s_x.at[hops], r_x.at[hops], other)

    def b_loc(hops, u, which_core):
        ref = piece(block_at(hops, which_core), third_of(u))
        return remote(ref, ref, s_loc.at[3 * hops + u], r_loc.at[3 * hops + u], mate)

    for u in range(2):
        loads[u].wait()
        g_ring(0, u).start()
        g_loc(0, u, core).start()
    loads[2].wait()
    for u in range(3):
        b_loc(0, u, core).start()

    def g_step(s, carry):
        for u in range(2):
            g_arrived(s, u).wait_recv()

            @pl.when(s < nc - 1)
            def _():
                g_ring(s, u).start()

            g_loc(s, u, core).start()
        return carry

    lax.fori_loop(1, nc, g_step, 0)
    for u in range(2):
        b_ring(0, u, 0).start()

    def g_local(s, carry):
        for u in range(2):
            g_loc(s, u, mate_core).wait_recv()
        return carry

    lax.fori_loop(0, nc, g_local, 0)

    per = tile_of(2 * nc, max(1, 256 // kb))
    tiles = 2 * nc // per

    def project(i, carry):
        f = i // tiles
        j = lax.rem(i, tiles)
        g = green[pl.ds(j * per, per), f].reshape(per * kb, nb)
        res = lax.dot_general(full[me], g, NT, preferred_element_type=jnp.float32)
        proj[f, :, pl.ds(pl.multiple_of(j * per * kb, 128), per * kb)] = res.astype(jnp.bfloat16)
        return carry

    lax.fori_loop(0, 2 * tiles, project, 0)
    acc[...] = jnp.zeros_like(acc)

    tile = tile_of(rows, 256)

    def compute(b):
        def one(i, carry):
            sub = full[b, pl.ds(pl.multiple_of(i * tile, 16), tile), :]
            occ = lax.dot_general(proj[0], sub, NT, preferred_element_type=jnp.float32)
            emp = lax.dot_general(proj[1], sub, NT, preferred_element_type=jnp.float32)
            product = (occ * emp).astype(jnp.bfloat16)
            acc[...] += jnp.dot(product, sub, preferred_element_type=jnp.float32)
            return carry

        lax.fori_loop(0, rows // tile, one, 0)

    def step(s, carry):
        @pl.when(s < nc)
        def _():
            b_ring(s - 1, 0, s).wait_recv()

            @pl.when(s < nc - 1)
            def _():
                b_ring(s, 0, s).start()

            b_x(s, 0).start()
            b_loc(s, 0, core).start()

        @pl.when(s > 1)
        def _():
            b_x(s - 1, 2).wait_recv()
            b_loc(s - 1, 2, core).start()

        compute(block_at(s - 1, core))

        @pl.when(s < nc)
        def _():
            b_ring(s - 1, 1, s).wait_recv()

            @pl.when(s < nc - 1)
            def _():
                b_ring(s, 1, s).start()

            b_loc(s, 1, core).start()

        for u in range(3):
            b_loc(s - 1, u, mate_core).wait_recv()
        compute(block_at(s - 1, mate_core))
        return carry

    lax.fori_loop(1, nc + 1, step, 0)

    cper = tile_of(nc, max(1, 128 // kb))
    ctiles = nc // cper

    def coef_copy(j):
        q = pl.ds(j * cper, cper)
        return remote(part.at[mate_core, q], half.at[q], cs_sem.at[j], cr_sem.at[j], mate)

    def coef(j, carry):
        cols = 2 * cper * kb
        back = acc[:, pl.ds(pl.multiple_of(j * cols, 128), cols)].astype(jnp.bfloat16)
        res = lax.dot_general(back, full[me], TN, preferred_element_type=jnp.float32)
        for i in range(2 * cper):
            part[i % 2, j * cper + i // 2] = res[i * kb:(i + 1) * kb]
        coef_copy(j).start()
        return carry

    lax.fori_loop(0, ctiles, coef, 0)

    def coef_wait(j, carry):
        coef_copy(j).wait_recv()
        q = pl.ds(j * cper, cper)
        part[core, q] = part[core, q] + half[q]
        return carry

    lax.fori_loop(0, ctiles, coef_wait, 0)

    hk = kb // 2

    def rs_copy(s, u):
        q = chip_at(pos - step_dir * (1 + s))
        return remote(
            part.at[core, q, pl.ds(u * hk, hk)], sums.at[s, pl.ds(u * hk, hk)],
            ss_sem.at[2 * s + u], sr_sem.at[2 * s + u], nxt,
        )

    for u in range(2):
        rs_copy(0, u).start()

    def rs_step(s, carry):
        q = chip_at(pos - step_dir * (1 + s))
        for u in range(2):
            rs_copy(s - 1, u).wait_recv()
            span = pl.ds(u * hk, hk)
            part[core, q, span] = part[core, q, span] + sums[s - 1, span]
            rs_copy(s, u).start()
        return carry

    lax.fori_loop(1, nc - 1, rs_step, 0)

    def tm_copy(u):
        span = pl.ds(u * hk, hk)
        return remote(part.at[core, chip, span], twin.at[span], ts_sem.at[u], tr_sem.at[u], other)

    for u in range(2):
        rs_copy(nc - 2, u).wait_recv()
        span = pl.ds(u * hk, hk)
        part[core, chip, span] = part[core, chip, span] + sums[nc - 2, span]
        tm_copy(u).start()
    scale = 1.0 / nr
    for u in range(2):
        tm_copy(u).wait_recv()
        span = pl.ds(u * hk, hk)
        mine = w_ref[tm, tm] * part[core, chip, span]
        out_ref[0, span] = scale * (mine + w_ref[tm, 1 - tm] * twin[span])

    def drain(s, carry):
        for u in range(2):
            @pl.when(s < nc - 1)
            def _():
                g_ring(s, u).wait_send()
                b_ring(s, u, s).wait_send()
                rs_copy(s, u).wait_send()

            g_loc(s, u, core).wait_send()
        for u in range(3):
            b_loc(s, u, core).wait_send()

        @pl.when(s > 0)
        def _():
            b_x(s, 0).wait_send()

        return carry

    lax.fori_loop(0, nc, drain, 0)

    def drain_coef(j, carry):
        coef_copy(j).wait_send()
        return carry

    lax.fori_loop(0, ctiles, drain_coef, 0)
    for u in range(2):
        tm_copy(u).wait_send()


def shards(occupied_green, empty_green, basis, time_weights):
    n = lax.axis_size("grid")
    nc = n // 2
    rows, nb = basis.shape
    kb = occupied_green.shape[1]
    dma = pltpu.SemaphoreType.DMA
    sizes = [3, 2 * nc, 2 * nc, 2 * nc, 2 * nc, 2 * nc, 2 * nc, nc, nc, 3 * nc, 3 * nc]
    sizes += [nc, nc, 2 * nc, 2 * nc, 2, 2]
    any_space = pl.BlockSpec(memory_space=pl.ANY)
    return pl.pallas_call(
        functools.partial(kernel, nc, n * rows),
        out_shape=jax.ShapeDtypeStruct((1, kb, nb), jnp.float32),
        in_specs=[any_space, any_space, any_space, pl.BlockSpec(memory_space=pltpu.SMEM)],
        out_specs=pl.BlockSpec(memory_space=pltpu.VMEM),
        scratch_shapes=[
            pltpu.VMEM((n, rows, nb), jnp.bfloat16),
            pltpu.VMEM((n, 2, kb, nb), jnp.bfloat16),
            pltpu.VMEM((2, rows, nb), jnp.bfloat16),
            pltpu.VMEM((rows, nb), jnp.float32),
            pltpu.VMEM((2, nc, kb, nb), jnp.float32),
            pltpu.VMEM((nc, kb, nb), jnp.float32),
            pltpu.VMEM((nc - 1, kb, nb), jnp.float32),
            pltpu.VMEM((kb, nb), jnp.float32),
        ]
        + [dma((k,)) for k in sizes],
        compiler_params=pltpu.CompilerParams(
            collective_id=0, has_side_effects=True, vmem_limit_bytes=67043328
        ),
    )(occupied_green, empty_green, basis, time_weights)


def solution(mesh):
    in_specs = (P("tm", "grid", None), P("tm", "grid", None), P("grid", None), P())
    out_specs = P("tm", "grid", None)
    return jax.shard_map(shards, mesh=mesh, in_specs=in_specs, out_specs=out_specs, check_vma=False)
```

time: 432 us -> 170 us (0.39)
  waiting for transfers between devices: 259 us -> 0 us
  Pallas kernels: 0 us -> 168 us
  matrix products: 153 us -> 0 us
  between operations: 13.2 us -> 0.01 us
    all_gather x2 -> x0, waiting for transfers between devices: 171 us -> none  [the longest x1 118 us: shards(): lax.all_gather(basis, 'grid', axis=0, tiled=True)]
    pallas_call x0 -> x1, Pallas kernels: none -> 168 us  [shards(): pl.pallas_call(functools.partial(kernel, nc, n * rows), out_shape=jax.Sha...]
    dot_general x14 -> x0, matrix products: 153 us -> none  [the longest x6 69.8 us: one_step(): jnp.dot(product, basis_subpart, preferred_element_type=jnp.float32)]
    reduce_scatter x2 -> x0, waiting for transfers between devices: 86.6 us -> none  [the longest x1 72.7 us: shards(): lax.psum_scatter(jnp.einsum('tsk,sl->ktl', back_half, basis, preferred_el...]
  transfers between devices with their start and end apart: 4 -> 0, of which waited for: 4 -> 0; matrix products, arithmetic and copies ran while one was open for 3% -> 0% of each run, Pallas kernels for 0% -> 0%
where the time goes in v1:
time: 170 us
  Pallas kernels  168 us (99%)
    pallas_call x1, Pallas kernels, shards(): pl.pallas_call(functools.partial(kernel, nc, n * rows), out_shape=jax.Sha...  168 us

profile of v1, /device:TPU:0, one launch (start us, length us, event | category | flops | bytes accessed | tf_op | source)
XLA Modules:
  0.0 169.9 jit_solution(15440563079440727212)
XLA Ops:
  0.0 168.2 %shard_map.46 = f32[1,64,1024]{2,1,0:T(8,128)} custom-call(bf16[1,64,1024]{2,1,0:T(8,128)(2,1)} %occ_ref.1, bf16[1,64,1024]{2,1,0:T(8,128)(2,1)} %emp_ref.1, bf16[768,1024]{1,0:T(8,128)(2,1)} %basis_ref.1, f32[2,2]{1,0:T(2,128)} %w_ref.1), custom_call_target="tpu_custom_call" | custom-call | tf_op jit(solution)/shard_map/pallas_call | solution.py:300
  168.2 1.7 copy.6

commit v2 on v1

--- a/solution.py
+++ b/solution.py
@@ -18,7 +18,7 @@
 
 def kernel(
     nc, nr, occ_ref, emp_ref, basis_ref, w_ref, out_ref,
-    full, green, proj, acc, part, half, sums, twin,
+    full, green, proj, acc, back, part, half, sums, twin,
     load_sem, gs_ring, gr_ring, gs_loc, gr_loc,
     s_ring, r_ring, s_x, r_x, s_loc, r_loc,
     cs_sem, cr_sem, ss_sem, sr_sem, ts_sem, tr_sem,
@@ -82,12 +82,22 @@
         )
 
     third = rows // 3
+    nh = nc // 2
 
     def piece(b, t):
         return full.at[b, pl.ds(pl.multiple_of(t * third, 16), third)]
 
     def third_of(u):
         return (2 * tm, 1, 2 - 2 * tm)[u]
+
+    chunk = max(16, 2 * third // nc)
+    per_unit = third // chunk
+
+    def own_chunk(c):
+        u = c // per_unit
+        first = (2 * tm * (1 - u) + u) * third + lax.rem(c, per_unit) * chunk
+        ref = full.at[me, pl.ds(pl.multiple_of(first, 16), chunk)]
+        remote(ref, ref, s_ring.at[u], r_ring.at[u], nxt).start()
 
     def b_ring(hops, u, src_hops):
         ref = piece(block_at(src_hops, core), third_of(u))
@@ -108,6 +118,7 @@
     loads[2].wait()
     for u in range(3):
         b_loc(0, u, core).start()
+    own_chunk(jnp.int32(0))
 
     def g_step(s, carry):
         for u in range(2):
@@ -118,11 +129,28 @@
                 g_ring(s, u).start()
 
             g_loc(s, u, core).start()
+
+        @pl.when(s < 2 * per_unit)
+        def _():
+            own_chunk(s)
+
         return carry
 
     lax.fori_loop(1, nc, g_step, 0)
+
+    def ring_in(s, u):
+        b_ring(s - 1, u, s).wait_recv()
+
+        @pl.when(s < nh)
+        def _():
+            b_ring(s, u, s).start()
+            b_loc(s, u, core).start()
+
+        if u == 0:
+            b_x(s, 0).start()
+
     for u in range(2):
-        b_ring(0, u, 0).start()
+        ring_in(1, u)
 
     def g_local(s, carry):
         for u in range(2):
@@ -134,65 +162,68 @@
     per = tile_of(2 * nc, max(1, 256 // kb))
     tiles = 2 * nc // per
 
-    def project(i, carry):
+    def project(b, i):
         f = i // tiles
         j = lax.rem(i, tiles)
         g = green[pl.ds(j * per, per), f].reshape(per * kb, nb)
-        res = lax.dot_general(full[me], g, NT, preferred_element_type=jnp.float32)
+        res = lax.dot_general(full[b], g, NT, preferred_element_type=jnp.float32)
         proj[f, :, pl.ds(pl.multiple_of(j * per * kb, 128), per * kb)] = res.astype(jnp.bfloat16)
-        return carry
-
-    lax.fori_loop(0, 2 * tiles, project, 0)
-    acc[...] = jnp.zeros_like(acc)
-
-    tile = tile_of(rows, 256)
+
+
+    tile = tile_of(rows, 768)
+
+    def terms(sub):
+        occ = lax.dot_general(proj[0], sub, NT, preferred_element_type=jnp.float32)
+        emp = lax.dot_general(proj[1], sub, NT, preferred_element_type=jnp.float32)
+        product = (occ * emp).astype(jnp.bfloat16)
+        acc[...] += jnp.dot(product, sub, preferred_element_type=jnp.float32)
 
     def compute(b):
-        def one(i, carry):
-            sub = full[b, pl.ds(pl.multiple_of(i * tile, 16), tile), :]
-            occ = lax.dot_general(proj[0], sub, NT, preferred_element_type=jnp.float32)
-            emp = lax.dot_general(proj[1], sub, NT, preferred_element_type=jnp.float32)
-            product = (occ * emp).astype(jnp.bfloat16)
-            acc[...] += jnp.dot(product, sub, preferred_element_type=jnp.float32)
+        for i in range(rows // tile):
+            terms(full[b, i * tile:(i + 1) * tile])
+
+    def rows_of(which, carry):
+        b = block_at(which * nh, core)
+
+        @pl.when(which == 1)
+        def _():
+            b_x(nh, 2).wait_recv()
+
+        lax.fori_loop(0, 2 * tiles, lambda i, c: (project(b, i), c)[1], 0)
+        acc[...] = jnp.zeros_like(acc)
+
+        def step(s, carry):
+            first = which == 0
+
+            @pl.when(first & (s > 0))
+            def _():
+                b_x(s, 2).wait_recv()
+                b_loc(s, 2, core).start()
+
+            compute(block_at(s, core))
+
+            @pl.when(first & (s < nh - 1))
+            def _():
+                ring_in(s + 2, 0)
+
+            @pl.when(first)
+            def _():
+                for u in range(3):
+                    b_loc(s, u, mate_core).wait_recv()
+
+            compute(block_at(s, mate_core))
+
+            @pl.when(first & (s < nh - 1))
+            def _():
+                ring_in(s + 2, 1)
+
             return carry
 
-        lax.fori_loop(0, rows // tile, one, 0)
-
-    def step(s, carry):
-        @pl.when(s < nc)
-        def _():
-            b_ring(s - 1, 0, s).wait_recv()
-
-            @pl.when(s < nc - 1)
-            def _():
-                b_ring(s, 0, s).start()
-
-            b_x(s, 0).start()
-            b_loc(s, 0, core).start()
-
-        @pl.when(s > 1)
-        def _():
-            b_x(s - 1, 2).wait_recv()
-            b_loc(s - 1, 2, core).start()
-
-        compute(block_at(s - 1, core))
-
-        @pl.when(s < nc)
-        def _():
-            b_ring(s - 1, 1, s).wait_recv()
-
-            @pl.when(s < nc - 1)
-            def _():
-                b_ring(s, 1, s).start()
-
-            b_loc(s, 1, core).start()
-
-        for u in range(3):
-            b_loc(s - 1, u, mate_core).wait_recv()
-        compute(block_at(s - 1, mate_core))
-        return carry
-
-    lax.fori_loop(1, nc + 1, step, 0)
+        lax.fori_loop(0, nh, step, 0)
+        back[which] = acc[...].astype(jnp.bfloat16)
+        return carry
+
+    lax.fori_loop(0, 2, rows_of, 0)
 
     cper = tile_of(nc, max(1, 128 // kb))
     ctiles = nc // cper
@@ -203,8 +234,10 @@
 
     def coef(j, carry):
         cols = 2 * cper * kb
-        back = acc[:, pl.ds(pl.multiple_of(j * cols, 128), cols)].astype(jnp.bfloat16)
-        res = lax.dot_general(back, full[me], TN, preferred_element_type=jnp.float32)
+        span = pl.ds(pl.multiple_of(j * cols, 128), cols)
+        res = lax.dot_general(back[0, :, span], full[me], TN, preferred_element_type=jnp.float32)
+        far = full[block_at(nh, core)]
+        res += lax.dot_general(back[1, :, span], far, TN, preferred_element_type=jnp.float32)
         for i in range(2 * cper):
             part[i % 2, j * cper + i // 2] = res[i * kb:(i + 1) * kb]
         coef_copy(j).start()
@@ -220,21 +253,22 @@
 
     lax.fori_loop(0, ctiles, coef_wait, 0)
 
-    hk = kb // 2
+    units = min(4, kb // 8)
+    hk = kb // units
 
     def rs_copy(s, u):
         q = chip_at(pos - step_dir * (1 + s))
         return remote(
             part.at[core, q, pl.ds(u * hk, hk)], sums.at[s, pl.ds(u * hk, hk)],
-            ss_sem.at[2 * s + u], sr_sem.at[2 * s + u], nxt,
+            ss_sem.at[units * s + u], sr_sem.at[units * s + u], nxt,
         )
 
-    for u in range(2):
+    for u in range(units):
         rs_copy(0, u).start()
 
     def rs_step(s, carry):
         q = chip_at(pos - step_dir * (1 + s))
-        for u in range(2):
+        for u in range(units):
             rs_copy(s - 1, u).wait_recv()
             span = pl.ds(u * hk, hk)
             part[core, q, span] = part[core, q, span] + sums[s - 1, span]
@@ -247,13 +281,13 @@
         span = pl.ds(u * hk, hk)
         return remote(part.at[core, chip, span], twin.at[span], ts_sem.at[u], tr_sem.at[u], other)
 
-    for u in range(2):
+    for u in range(units):
         rs_copy(nc - 2, u).wait_recv()
         span = pl.ds(u * hk, hk)
         part[core, chip, span] = part[core, chip, span] + sums[nc - 2, span]
         tm_copy(u).start()
     scale = 1.0 / nr
-    for u in range(2):
+    for u in range(units):
         tm_copy(u).wait_recv()
         span = pl.ds(u * hk, hk)
         mine = w_ref[tm, tm] * part[core, chip, span]
@@ -264,16 +298,20 @@
             @pl.when(s < nc - 1)
             def _():
                 g_ring(s, u).wait_send()
+
+            g_loc(s, u, core).wait_send()
+        for u in range(units):
+            @pl.when(s < nc - 1)
+            def _():
+                rs_copy(s, u).wait_send()
+
+        @pl.when(s < nh)
+        def _():
+            for u in range(2):
                 b_ring(s, u, s).wait_send()
-                rs_copy(s, u).wait_send()
-
-            g_loc(s, u, core).wait_send()
-        for u in range(3):
-            b_loc(s, u, core).wait_send()
-
-        @pl.when(s > 0)
-        def _():
-            b_x(s, 0).wait_send()
+            for u in range(3):
+                b_loc(s, u, core).wait_send()
+            b_x(s + 1, 0).wait_send()
 
         return carry
 
@@ -284,7 +322,7 @@
         return carry
 
     lax.fori_loop(0, ctiles, drain_coef, 0)
-    for u in range(2):
+    for u in range(units):
         tm_copy(u).wait_send()
 
 
@@ -295,7 +333,7 @@
     kb = occupied_green.shape[1]
     dma = pltpu.SemaphoreType.DMA
     sizes = [3, 2 * nc, 2 * nc, 2 * nc, 2 * nc, 2 * nc, 2 * nc, nc, nc, 3 * nc, 3 * nc]
-    sizes += [nc, nc, 2 * nc, 2 * nc, 2, 2]
+    sizes += [nc, nc, 4 * nc, 4 * nc, 4, 4]
     any_space = pl.BlockSpec(memory_space=pl.ANY)
     return pl.pallas_call(
         functools.partial(kernel, nc, n * rows),
@@ -307,6 +345,7 @@
             pltpu.VMEM((n, 2, kb, nb), jnp.bfloat16),
             pltpu.VMEM((2, rows, nb), jnp.bfloat16),
             pltpu.VMEM((rows, nb), jnp.float32),
+            pltpu.VMEM((2, rows, nb), jnp.bfloat16),
             pltpu.VMEM((2, nc, kb, nb), jnp.float32),
             pltpu.VMEM((nc, kb, nb), jnp.float32),
             pltpu.VMEM((nc - 1, kb, nb), jnp.float32),

time: 170 us -> 158 us (0.929)
  Pallas kernels: 168 us -> 156 us
    pallas_call x1, Pallas kernels: 168 us -> 156 us  [shards(): pl.pallas_call(functools.partial(kernel, nc, n * rows), out_shape=jax.Sha...]
where the time goes in v2:
time: 158 us
  Pallas kernels  156 us (99%)
  local copies, waits for them, and re-layouts  1.67 us (1%)
    pallas_call x1, Pallas kernels, shards(): pl.pallas_call(functools.partial(kernel, nc, n * rows), out_shape=jax.Sha...  156 us

profile of v2, /device:TPU:0, one launch (start us, length us, event | category | flops | bytes accessed | tf_op | source)
XLA Modules:
  0.0 157.6 jit_solution(6209729749375389007)
XLA Ops:
  0.0 156.0 %shard_map.46 = f32[1,64,1024]{2,1,0:T(8,128)} custom-call(bf16[1,64,1024]{2,1,0:T(8,128)(2,1)} %occ_ref.1, bf16[1,64,1024]{2,1,0:T(8,128)(2,1)} %emp_ref.1, bf16[768,1024]{1,0:T(8,128)(2,1)} %basis_ref.1, f32[2,2]{1,0:T(2,128)} %w_ref.1), custom_call_target="tpu_custom_call" | custom-call | tf_op jit(solution)/shard_map/pallas_call | solution.py:338
  156.0 1.7 %copy.6 = f32[1,64,1024]{2,1,0:T(8,128)} copy(f32[1,64,1024]{2,1,0:T(8,128)} %shard_map.46) | data formatting | bytes 524288

commit v3 on v2

--- a/solution.py
+++ b/solution.py
@@ -159,7 +159,7 @@
 
     lax.fori_loop(0, nc, g_local, 0)
 
-    per = tile_of(2 * nc, max(1, 256 // kb))
+    per = tile_of(2 * nc, max(1, 512 // kb))
     tiles = 2 * nc // per
 
     def project(b, i):
@@ -225,7 +225,7 @@
 
     lax.fori_loop(0, 2, rows_of, 0)
 
-    cper = tile_of(nc, max(1, 128 // kb))
+    cper = tile_of(nc, max(1, 256 // kb))
     ctiles = nc // cper
 
     def coef_copy(j):

time: 158 us -> 157 us (level)
  no operation moved by 1% of the time
where the time goes in v3:
time: 157 us; the launch traced here: 156 us
  Pallas kernels  155 us (99%)
  local copies, waits for them, and re-layouts  1.67 us (1%)
    pallas_call x1, Pallas kernels, shards(): pl.pallas_call(functools.partial(kernel, nc, n * rows), out_shape=jax.Sha...  155 us

profile of v3, /device:TPU:0, one launch (start us, length us, event | category | flops | bytes accessed | tf_op | source)
XLA Modules:
  0.0 156.4 jit_solution(8003356514895276142)
XLA Ops:
  0.0 154.8 %shard_map.46 = f32[1,64,1024]{2,1,0:T(8,128)} custom-call(bf16[1,64,1024]{2,1,0:T(8,128)(2,1)} %occ_ref.1, bf16[1,64,1024]{2,1,0:T(8,128)(2,1)} %emp_ref.1, bf16[768,1024]{1,0:T(8,128)(2,1)} %basis_ref.1, f32[2,2]{1,0:T(2,128)} %w_ref.1), custom_call_target="tpu_custom_call" | custom-call | tf_op jit(solution)/shard_map/pallas_call | solution.py:338
  154.8 1.7 %copy.6 = f32[1,64,1024]{2,1,0:T(8,128)} copy(f32[1,64,1024]{2,1,0:T(8,128)} %shard_map.46) | data formatting | bytes 524288
